TPU v7x, 256 devices: a whole 4x4x8 slice. The times are simulated.
256 devices in a mesh: dp: 16 (over z, core), frame: 16 (over y, x).
Axes of the slice: x: 4, y: 4, z: 8, core: 2. Of those that a mesh axis runs over, the one named last changes fastest.
Arguments:
- latents: bfloat16 [16, 16, 512, 640], P('dp', 'frame'), may hold values from -6 to 6
- cotangent: bfloat16 [16, 16, 512, 640], P('dp', 'frame'), may hold values from -6 to 6
- timesteps: int32 [16], P('dp'), may hold values from 0 to 999
- spatial_weight: bfloat16 [9, 640, 640], replicated, may hold values from -0.078125 to 0.078125
- temporal_weight: bfloat16 [3, 640, 640], replicated, may hold values from -0.125 to 0.125
Outputs:
- new_spatial: float32 [9, 640, 640], P(None, 'frame')
- new_temporal: float32 [3, 640, 640], P(None, 'frame')
All inputs are finite; a program needn't handle non-finite values.
Results may differ from a plain program's by a relative error of at most 0.02.
Values may be sent and summed in bfloat16 or wider, within the bound.
No kernel may reach another device: no remote copies, remote signals or barrier semaphores. Data moves between devices by JAX's collectives and lax.ppermute only.
A program may use at most 128 MiB of HBM per device.

v0:
```python
import math
import jax
import jax.numpy as jnp
from jax import lax
from jax.sharding import PartitionSpec as P

WIDTH = 64
SLAB = 8


def embed(timesteps, channels):
    half_width = channels // 2
    frequencies = jnp.exp(
        -math.log(10000.0) * jnp.arange(half_width, dtype=jnp.float32) / half_width
    )
    angles = timesteps.astype(jnp.float32)[:, None] * frequencies[None, :]
    return jnp.concatenate([jnp.sin(angles), jnp.cos(angles)], axis=1)


def unfold(activated, slab_rows, grid_width):
    lead_count, pixels, channels = activated.shape
    grid_cells = activated.reshape(lead_count, slab_rows, grid_width, channels)
    padded = jnp.pad(grid_cells, ((0, 0), (1, 1), (1, 1), (0, 0)))
    pieces = [
        padded[:, row_off : row_off + slab_rows, col_off : col_off + grid_width, :]
        for row_off in range(3)
        for col_off in range(3)
    ]
    return jnp.concatenate(pieces, axis=3).reshape(lead_count, pixels, 9 * channels)


def silu_slope(pre_act):
    logistic = jax.nn.sigmoid(pre_act)
    return logistic * (1.0 + pre_act * (1.0 - logistic))


def clip_factor(squares, channels):
    max_norm = 0.5 * math.sqrt(12.0) * channels
    return jnp.minimum(1.0, max_norm / (jnp.sqrt(squares) + 1e-06))


def temporal(gated_pad, cot_pad, cot_here, weight):
    frames_here = cot_here.shape[1]
    channels = cot_here.shape[3]
    cot_rows = cot_here.reshape(-1, channels)
    weight_grads = []
    grad_gated = jnp.zeros(cot_rows.shape, jnp.float32)
    for offset in range(3):
        gated_rows = gated_pad[:, offset : offset + frames_here].reshape(-1, channels)
        weight_grads.append(
            jnp.einsum("rc,rd->cd", gated_rows, cot_rows, preferred_element_type=jnp.float32)
        )
        shifted = cot_pad[:, 2 - offset : 2 - offset + frames_here].reshape(-1, channels)
        grad_gated = grad_gated + jnp.einsum(
            "rd,cd->rc", shifted, weight[offset], preferred_element_type=jnp.float32
        )
    return (jnp.stack(weight_grads), grad_gated.astype(jnp.bfloat16).reshape(cot_here.shape))


def owned_step(spatial_weight, temporal_weight, spatial_part, temporal_part, factor):
    rows_each = spatial_part.shape[1]
    cols_each = spatial_part.shape[2]
    row_start = lax.axis_index("frame") * rows_each
    spatial_here = lax.dynamic_slice(spatial_weight, (0, row_start, 0), (9, rows_each, cols_each))
    temporal_here = lax.dynamic_slice(temporal_weight, (0, row_start, 0), (3, rows_each, cols_each))
    new_spatial = spatial_here.astype(jnp.float32) - factor * spatial_part
    new_temporal = temporal_here.astype(jnp.float32) - factor * temporal_part
    return (new_spatial, new_temporal)


def on_device(latents, cotangent, timesteps, spatial_weight, temporal_weight):
    channels = latents.shape[3]
    pixels = latents.shape[2]
    shifts = embed(timesteps, channels)
    activated = jax.nn.silu(latents.astype(jnp.float32) + shifts[:, None, None, :]).astype(
        jnp.bfloat16
    )
    columns = unfold(activated.reshape(-1, pixels, channels), SLAB, WIDTH).reshape(-1, 9 * channels)
    pre_act = jnp.dot(
        columns, spatial_weight.reshape(9 * channels, channels), preferred_element_type=jnp.float32
    )
    gated = jax.nn.silu(pre_act).astype(jnp.bfloat16).reshape(latents.shape)
    pad_spec = ((0, 0), (1, 1), (0, 0), (0, 0))
    gated_rows, cot_rows = (
        lax.all_to_all(gated, "frame", split_axis=2, concat_axis=1, tiled=True),
        lax.all_to_all(cotangent, "frame", split_axis=2, concat_axis=1, tiled=True),
    )
    temporal_grad, grad_rows = temporal(
        jnp.pad(gated_rows, pad_spec), jnp.pad(cot_rows, pad_spec), cot_rows, temporal_weight
    )
    grad_gated = lax.all_to_all(grad_rows, "frame", split_axis=1, concat_axis=2, tiled=True)
    grad_pre = (
        grad_gated.reshape(pixels, channels).astype(jnp.float32) * silu_slope(pre_act)
    ).astype(jnp.bfloat16)
    spatial_grad = jnp.einsum(
        "rk,rc->kc", columns, grad_pre, preferred_element_type=jnp.float32
    ).reshape(9, channels, channels)
    spatial_part = lax.psum_scatter(
        spatial_grad.astype(jnp.bfloat16), "frame", scatter_dimension=1, tiled=True
    ).astype(jnp.float32)
    temporal_part = lax.psum_scatter(
        temporal_grad.astype(jnp.bfloat16), "frame", scatter_dimension=1, tiled=True
    ).astype(jnp.float32)
    spatial_part, temporal_part = (
        lax.psum(spatial_part.astype(jnp.bfloat16), "dp").astype(jnp.float32),
        lax.psum(temporal_part.astype(jnp.bfloat16), "dp").astype(jnp.float32),
    )
    squares = lax.psum(
        jnp.sum(spatial_part * spatial_part) + jnp.sum(temporal_part * temporal_part), "frame"
    )
    factor = clip_factor(squares, channels)
    return owned_step(spatial_weight, temporal_weight, spatial_part, temporal_part, factor)


def solution(mesh):
    in_specs = (P("dp", "frame", None, None), P("dp", "frame", None, None), P("dp"), P(), P())
    out_specs = (P(None, "frame", None), P(None, "frame", None))
    return jax.shard_map(
        on_device, mesh=mesh, in_specs=in_specs, out_specs=out_specs, check_vma=False
    )
```

profile of v0, /device:TPU:0, one launch (start us, length us, event | category | flops | bytes accessed | tf_op | source)
XLA Modules:
  0.0 435.5 jit_solution(13196924805992825364)
XLA Ops:
  7.2 2.1 copy.27
  9.3 0.0 copy-start.1
  9.3 0.6 broadcast.49
  9.9 4.7 %reduce.2 = bf16[512,640]{1,0:T(8,128)(2,1)S(1)} reduce(bf16[512,1,1,640]{3,2,1,0:T(2,128)(2,1)S(1)} %bitcast.81, bf16[]{:T(256)} %broadcast.49), dimensions={1,2}, to_apply=%bitcast.78.reduce_sub_computation | reduce | bytes 1310722
  14.6 1.0 reshape.109
  15.5 5.3 %all-to-all-start = ((bf16[16,2,10240]{2,1,0:T(2,128)(2,1)}), bf16[16,2,10240]{2,1,0:T(2,128)(2,1)S(1)}, u32[]{:S(2)}, u32[]{:S(2)}) async-start(bf16[16,2,10240]{2,1,0:T(2,128)(2,1)} %reshape.109), calls=%async_computation | async-start | bytes 1310720 | tf_op jit(solution)/shard_map/all_to_all | solution.py:86
  21.5 0.1 fusion.23
  21.6 0.1 maximum_reduce_fusion
  21.7 0.0 copy-done.1
  21.7 0.4 multiply_convert_fusion.1
  22.1 1.6 pad_slice_fusion
  23.7 0.9 constant_dynamic-update-slice_fusion.7
  24.6 0.9 constant_dynamic-update-slice_fusion.6
  25.5 0.9 constant_dynamic-update-slice_fusion.5
  26.5 0.9 constant_dynamic-update-slice_fusion.4
  27.4 6.4 %all-to-all-done = bf16[16,2,10240]{2,1,0:T(2,128)(2,1)S(1)} async-done(((bf16[16,2,10240]{2,1,0:T(2,128)(2,1)}), bf16[16,2,10240]{2,1,0:T(2,128)(2,1)S(1)}, u32[]{:S(2)}, u32[]{:S(2)}) %all-to-all-start) | async-done | bytes 655392 | tf_op jit(solution)/shard_map/all_to_all | solution.py:86
  33.8 0.6 reshape.110
  34.4 0.0 copy-start
  34.5 0.1 copy.20
  34.6 0.1 pad_slice_fusion.10
  34.7 1.5 copy-done
  36.1 0.8 fusion.9
  36.9 0.8 convolution_add_fusion.1
  37.7 1.6 fusion
  39.4 0.0 copy-start.3
  39.4 4.6 %all-to-all-start.1 = ((bf16[1,16,32,640]{3,2,0,1:T(8,128)(2,1)}), bf16[1,16,32,640]{3,2,0,1:T(8,128)(2,1)}, u32[]{:S(2)}, u32[]{:S(2)}) async-start(bf16[1,16,32,640]{3,2,0,1:T(8,128)(2,1)} %bitcast.19), calls=%async_computation.1 | async-start | bytes 1310720 | tf_op jit(solution)/shard_map/all_to_all | solution.py:91
  44.0 1.3 bitcast_dynamic-update-slice_fusion
  45.2 2.1 constant_dynamic-update-slice_fusion.3
  47.3 0.0 copy-done.3
  47.3 1.0 constant_dynamic-update-slice_fusion.2
  48.3 0.0 copy-done.2
  48.3 1.0 constant_dynamic-update-slice_fusion.1
  49.3 1.0 constant_dynamic-update-slice_fusion
  50.3 8.4 %copy.12 = bf16[5760,512]{1,0:T(8,128)(2,1)} copy(bf16[5760,512]{0,1:T(8,128)(2,1)} %bitcast.11) | data formatting | bytes 11796480 | tf_op jit(solution)/shard_map/rk,rc->kc/dot_general | solution.py:95
  58.7 0.0 all-to-all-done.1
  58.7 9.8 %fusion.20 = (bf16[1,1,512,640]{3,2,1,0:T(8,128)(2,1)S(1)}, bf16[512,640]{1,0:T(8,128)(2,1)S(1)}) fusion(bf16[1,16,32,640]{3,2,0,1:T(8,128)(2,1)} %all-to-all-done.1, bf16[512,5760]{1,0:T(8,128)(2,1)} %constant_dynamic-update-slice_fusion, bf16[5760,640]{1,0:T(8,128)(2,1)} %bitcast.99), kind=kOutput, calls=%fused_computation.46 | convolution fusion | flops 3778805760 | bytes 15237120 | tf_op jit(solution)/shard_map/dot_general | solution.py:79
  68.5 1.0 copy.26
  69.5 4.7 %reduce.3 = bf16[512,640]{1,0:T(8,128)(2,1)S(1)} reduce(bf16[512,1,1,640]{3,2,1,0:T(2,128)(2,1)S(1)} %bitcast.82, bf16[]{:T(256)} %broadcast.49), dimensions={1,2}, to_apply=%bitcast.77.reduce_sub_computation | reduce | bytes 1310722
  74.2 1.0 reshape.111
  75.2 6.9 %all-to-all-start.2 = ((bf16[16,2,10240]{2,1,0:T(2,128)(2,1)}), bf16[16,2,10240]{2,1,0:T(2,128)(2,1)S(1)}, u32[]{:S(2)}, u32[]{:S(2)}) async-start(bf16[16,2,10240]{2,1,0:T(2,128)(2,1)} %reshape.111), calls=%async_computation.2 | async-start | bytes 1310720 | tf_op jit(solution)/shard_map/all_to_all | solution.py:85
  82.1 0.3 all-reduce.10.cloned.1.call-start
  82.4 10.4 %convolution_convert_fusion = bf16[9,640,640]{2,1,0:T(8,128)(2,1)} fusion(bf16[9,640,512]{2,1,0:T(8,128)(2,1)} %bitcast.79, bf16[512,640]{1,0:T(8,128)(2,1)S(1)} %get-tuple-element.7), kind=kOutput, calls=%fused_computation | convolution fusion | flops 3778560000 | bytes 13926400 | tf_op jit(solution)/shard_map/rk,rc->kc/dot_general | solution.py:95
  92.8 0.7 all-to-all-done.2
  93.5 0.6 reshape.112
  94.1 0.1 copy.22
  94.2 0.7 fusion.3
  94.9 0.1 pad_slice_fusion.9
  95.0 0.7 fusion.2
  95.7 0.7 fusion.4
  96.5 1.8 pad_maximum_fusion
  98.2 0.0 all-reduce.10.cloned.1.call-update
  98.3 0.0 all-reduce.12.cloned.1.call-start
  98.3 0.6 copy-done.4
  98.9 0.6 dynamic-slice
  100.1 164.3 %all-reduce.10.cloned.1.call-done = (bf16[9,640,640]{2,1,0:T(8,128)(2,1)}, bf16[3,640,640]{2,1,0:T(8,128)(2,1)}) async-done(((bf16[9,640,640]{2,1,0:T(8,128)(2,1)}, bf16[3,640,640]{2,1,0:T(8,128)(2,1)}), (bf16[9,640,640]{2,1,0:T(8,128)(2,1)}, bf16[3,640,640]{2,1,0:T(8,128)(2,1)})) %all-reduce.10.cloned.1.call-update) | async-done | bytes 9830416
  264.5 1.8 constant_dynamic-slice_fusion.1
  266.3 1.6 constant_dynamic-slice_fusion
  267.9 0.0 all-reduce.12.cloned.1.call-update
  267.9 110.4 %all-reduce.12.cloned.1.call-done = (bf16[9,40,640]{2,1,0:T(8,128)(2,1)}, bf16[3,40,640]{2,1,0:T(8,128)(2,1)}) async-done(((bf16[9,40,640]{2,1,0:T(8,128)(2,1)}, bf16[3,40,640]{2,1,0:T(8,128)(2,1)}), (bf16[9,40,640]{2,1,0:T(8,128)(2,1)}, bf16[3,40,640]{2,1,0:T(8,128)(2,1)})) %all-reduce.12.cloned.1.call-update) | async-done | bytes 614416 | tf_op jit(solution)/shard_map/psum | solution.py:105
  378.3 1.6 fusion.21
  379.9 1.9 fusion.5
  383.1 40.8 %psum.23 = f32[]{:T(128)} all-reduce(f32[]{:T(128)S(6)} %add.63), channel_id=1, replica_groups=mesh['dp'=16,'frame'=16] {'frame'}, use_global_device_ids=true, to_apply=%region_6.7 | all-reduce | flops 1 | bytes 8 | tf_op jit(solution)/shard_map/psum | solution.py:108
  424.7 1.8 fusion.22
  426.4 2.2 fusion.6
  (2 shorter events, 0.0 us)
Async XLA Ops:
  9.3 12.4 %copy-start.1 = (bf16[1,1,512,640]{3,2,1,0:T(8,128)(2,1)S(1)}, bf16[1,1,512,640]{3,2,1,0:T(8,128)(2,1)}, u32[]{:S(2)}) copy-start(bf16[1,1,512,640]{3,2,1,0:T(8,128)(2,1)} %param.5) | copy-start | bytes 1966084
  15.5 18.3 %all-to-all-start = ((bf16[16,2,10240]{2,1,0:T(2,128)(2,1)}), bf16[16,2,10240]{2,1,0:T(2,128)(2,1)S(1)}, u32[]{:S(2)}, u32[]{:S(2)}) async-start(bf16[16,2,10240]{2,1,0:T(2,128)(2,1)} %reshape.109), calls=%async_computation | async-start | bytes 1310720 | tf_op jit(solution)/shard_map/all_to_all | solution.py:86
  34.4 1.7 copy-start
  39.4 7.9 %copy-start.3 = (bf16[1,8,64,640]{3,2,1,0:T(8,128)(2,1)S(1)}, bf16[1,8,64,640]{3,2,1,0:T(8,128)(2,1)}, u32[]{:S(2)}) copy-start(bf16[1,8,64,640]{3,2,1,0:T(8,128)(2,1)} %get-tuple-element.17) | copy-start | bytes 1966084
  39.4 9.0 %copy-start.2 = (bf16[1,8,64,640]{3,2,1,0:T(8,128)(2,1)S(1)}, bf16[1,8,64,640]{3,2,1,0:T(8,128)(2,1)}, u32[]{:S(2)}) copy-start(bf16[1,8,64,640]{3,2,1,0:T(8,128)(2,1)} %get-tuple-element.18) | copy-start | bytes 1966084
  39.4 19.3 %all-to-all-start.1 = ((bf16[1,16,32,640]{3,2,0,1:T(8,128)(2,1)}), bf16[1,16,32,640]{3,2,0,1:T(8,128)(2,1)}, u32[]{:S(2)}, u32[]{:S(2)}) async-start(bf16[1,16,32,640]{3,2,0,1:T(8,128)(2,1)} %bitcast.19), calls=%async_computation.1 | async-start | bytes 1310720 | tf_op jit(solution)/shard_map/all_to_all | solution.py:91
  75.2 18.3 %all-to-all-start.2 = ((bf16[16,2,10240]{2,1,0:T(2,128)(2,1)}), bf16[16,2,10240]{2,1,0:T(2,128)(2,1)S(1)}, u32[]{:S(2)}, u32[]{:S(2)}) async-start(bf16[16,2,10240]{2,1,0:T(2,128)(2,1)} %reshape.111), calls=%async_computation.2 | async-start | bytes 1310720 | tf_op jit(solution)/shard_map/all_to_all | solution.py:85
  82.1 182.3 %all-reduce.10.cloned.1.call-start = ((), (), s32[]{:S(2)}) async-start(), calls=%async_computation.3 | async-start | bytes 19660800
  98.2 0.7 copy-start.4
  98.3 280.1 %all-reduce.12.cloned.1.call-start = ((), (), s32[]{:S(2)}) async-start(), calls=%async_computation.4 | async-start | bytes 1228800 | tf_op jit(solution)/shard_map/psum | solution.py:105
Sparse Core Ops, SparseCore 0:
  98.4 166.0 all-reduce.9
  268.0 110.2 all-reduce.11
where the time goes:
time: 436 us; the launch traced here: 435 us
  waiting for transfers between devices  282 us (65%)
  blocking collectives  40.8 us (9%)
  local copies, waits for them, and re-layouts  32.2 us (7%)
  matrix products  25.6 us (6%)
  other arithmetic  20.3 us (5%)
  between operations  17.6 us (4%)
  starting transfers between devices  17.1 us (4%)
    unnamed x3, waiting for transfers between devices  164 us
    psum x1, waiting for transfers between devices, on_device(): lax.psum(spatial_part.astype(jnp.bfloat16), 'dp').astype(jnp.float32)  110 us
    psum x1, blocking collectives, on_device(): lax.psum(jnp.sum(spatial_part * spatial_part) + jnp.sum(temporal_part * t...  40.8 us
    unnamed x28, local copies, waits for them, and re-layouts  20 us
    unnamed x3, other arithmetic  10.6 us
    dot_general x1, matrix products, on_device(): jnp.einsum('rk,rc->kc', columns, grad_pre, preferred_element_type=jnp.flo...  10.4 us
    dot_general x1, matrix products, on_device(): jnp.dot(columns, spatial_weight.reshape(9 * channels, channels), preferre...  9.82 us
  transfers between devices with their start and end apart: 5, of which 4 were waited for; matrix products, arithmetic and copies ran while one was open for 7% of the time, Pallas kernels for 0%

commit v1 on v0

--- a/solution.py
+++ b/solution.py
@@ -102,7 +102,9 @@
         temporal_grad.astype(jnp.bfloat16), "frame", scatter_dimension=1, tiled=True
     ).astype(jnp.float32)
     spatial_part, temporal_part = (
-        lax.psum(spatial_part.astype(jnp.bfloat16), "dp").astype(jnp.float32),
+        jnp.sum(lax.all_gather(spatial_part.astype(jnp.bfloat16), "dp"), axis=0).astype(
+            jnp.float32
+        ),
         lax.psum(temporal_part.astype(jnp.bfloat16), "dp").astype(jnp.float32),
     )
     squares = lax.psum(

time: 436 us -> 481 us (1.10)
  waiting for transfers between devices: 282 us -> 323 us
    all_gather x0 -> x1, waiting for transfers between devices: none -> 50.9 us  [on_device(): lax.all_gather(spatial_part.astype(jnp.bfloat16), 'dp')]
    psum x1, waiting for transfers between devices: 110 us -> 101 us  [on_device(): lax.psum(temporal_part.astype(jnp.bfloat16), 'dp').astype(jnp.float32)]
    unnamed x3 -> x4, waiting for transfers between devices: 164 us -> 164 us
    unnamed x28 -> x30, local copies, waits for them, and re-layouts: 20 us -> 19.9 us
  transfers between devices with their start and end apart: 5 -> 6, of which waited for: 4 -> 5; matrix products, arithmetic and copies ran while one was open for 7% -> 7% of each run, Pallas kernels for 0% -> 0%
where the time goes in v1:
time: 481 us; the launch traced here: 480 us
  waiting for transfers between devices  323 us (67%)
  blocking collectives  40.8 us (8%)
  local copies, waits for them, and re-layouts  32.3 us (7%)
  matrix products  25.7 us (5%)
  other arithmetic  23.4 us (5%)
  between operations  17.3 us (4%)
  starting transfers between devices  17.2 us (4%)
    unnamed x4, waiting for transfers between devices  164 us
    psum x1, waiting for transfers between devices, on_device(): lax.psum(temporal_part.astype(jnp.bfloat16), 'dp').astype(jnp.float32)  101 us
    all_gather x1, waiting for transfers between devices, on_device(): lax.all_gather(spatial_part.astype(jnp.bfloat16), 'dp')  50.9 us
    psum x1, blocking collectives, on_device(): lax.psum(jnp.sum(spatial_part * spatial_part) + jnp.sum(temporal_part * t...  40.8 us
    unnamed x30, local copies, waits for them, and re-layouts  19.9 us
    unnamed x3, other arithmetic  10.5 us
    dot_general x1, matrix products, on_device(): jnp.einsum('rk,rc->kc', columns, grad_pre, preferred_element_type=jnp.flo...  10.5 us
    dot_general x1, matrix products, on_device(): jnp.dot(columns, spatial_weight.reshape(9 * channels, channels), preferre...  9.82 us
  transfers between devices with their start and end apart: 6, of which 5 were waited for; matrix products, arithmetic and copies ran while one was open for 7% of the time, Pallas kernels for 0%

profile of v1, /device:TPU:0, one launch (start us, length us, event | category | flops | bytes accessed | tf_op | source)
XLA Modules:
  0.0 480.2 jit_solution(2241347478761492666)
XLA Ops:
  7.2 2.1 copy.27
  9.3 0.0 copy-start.1
  9.3 0.5 broadcast.49
  9.8 4.6 reduce.3
  14.4 1.0 reshape.110
  15.4 5.3 %all-to-all-start = ((bf16[16,2,10240]{2,1,0:T(2,128)(2,1)}), bf16[16,2,10240]{2,1,0:T(2,128)(2,1)S(1)}, u32[]{:S(2)}, u32[]{:S(2)}) async-start(bf16[16,2,10240]{2,1,0:T(2,128)(2,1)} %reshape.110), calls=%async_computation | async-start | bytes 1310720 | tf_op jit(solution)/shard_map/all_to_all | solution.py:86
  21.4 0.1 fusion.23
  21.5 0.1 maximum_reduce_fusion
  21.6 0.4 multiply_convert_fusion.1
  22.0 1.6 pad_slice_fusion
  23.6 1.0 constant_dynamic-update-slice_fusion.7
  24.5 0.9 constant_dynamic-update-slice_fusion.6
  25.5 1.0 constant_dynamic-update-slice_fusion.5
  26.4 0.9 constant_dynamic-update-slice_fusion.4
  27.3 6.4 %all-to-all-done = bf16[16,2,10240]{2,1,0:T(2,128)(2,1)S(1)} async-done(((bf16[16,2,10240]{2,1,0:T(2,128)(2,1)}), bf16[16,2,10240]{2,1,0:T(2,128)(2,1)S(1)}, u32[]{:S(2)}, u32[]{:S(2)}) %all-to-all-start) | async-done | bytes 655392 | tf_op jit(solution)/shard_map/all_to_all | solution.py:86
  33.7 0.6 reshape.111
  34.3 0.0 copy-start
  34.4 0.1 copy.20
  34.5 0.1 pad_slice_fusion.10
  34.6 1.5 copy-done
  36.0 0.8 fusion.9
  36.8 0.8 convolution_add_fusion.1
  37.7 1.7 fusion
  39.3 4.6 all-to-all-start.1
  43.9 1.3 bitcast_dynamic-update-slice_fusion
  45.2 2.1 constant_dynamic-update-slice_fusion.3
  47.2 1.0 constant_dynamic-update-slice_fusion.2
  48.2 1.0 constant_dynamic-update-slice_fusion.1
  49.1 1.0 constant_dynamic-update-slice_fusion
  50.2 8.5 %copy.12 = bf16[5760,512]{1,0:T(8,128)(2,1)} copy(bf16[5760,512]{0,1:T(8,128)(2,1)} %bitcast.11) | data formatting | bytes 11796480 | tf_op jit(solution)/shard_map/rk,rc->kc/dot_general | solution.py:95
  58.7 0.0 all-to-all-done.1
  58.7 9.8 %fusion.20 = (bf16[1,1,512,640]{3,2,1,0:T(8,128)(2,1)S(1)}, bf16[512,640]{1,0:T(8,128)(2,1)S(1)}) fusion(bf16[1,16,32,640]{3,2,0,1:T(8,128)(2,1)} %all-to-all-done.1, bf16[512,5760]{1,0:T(8,128)(2,1)} %constant_dynamic-update-slice_fusion, bf16[5760,640]{1,0:T(8,128)(2,1)} %bitcast.101), kind=kOutput, calls=%fused_computation.46 | convolution fusion | flops 3778805760 | bytes 15237120 | tf_op jit(solution)/shard_map/dot_general | solution.py:79
  68.6 1.0 copy.26
  69.6 4.6 reduce.4
  74.2 1.0 reshape.112
  75.2 6.9 %all-to-all-start.2 = ((bf16[16,2,10240]{2,1,0:T(2,128)(2,1)}), bf16[16,2,10240]{2,1,0:T(2,128)(2,1)S(1)}, u32[]{:S(2)}, u32[]{:S(2)}) async-start(bf16[16,2,10240]{2,1,0:T(2,128)(2,1)} %reshape.112), calls=%async_computation.2 | async-start | bytes 1310720 | tf_op jit(solution)/shard_map/all_to_all | solution.py:85
  82.1 0.3 all-reduce.11.cloned.1.call-start
  82.4 10.5 %convolution_convert_fusion = bf16[9,640,640]{2,1,0:T(8,128)(2,1)} fusion(bf16[9,640,512]{2,1,0:T(8,128)(2,1)} %bitcast.81, bf16[512,640]{1,0:T(8,128)(2,1)S(1)} %get-tuple-element.5), kind=kOutput, calls=%fused_computation | convolution fusion | flops 3778560000 | bytes 13926400 | tf_op jit(solution)/shard_map/rk,rc->kc/dot_general | solution.py:95
  92.8 0.6 all-to-all-done.2
  93.4 0.6 reshape.113
  94.0 0.1 copy.22
  94.1 0.7 fusion.3
  94.9 0.1 pad_slice_fusion.9
  95.0 0.7 fusion.2
  95.7 0.7 fusion.4
  96.4 1.8 pad_maximum_fusion
  98.2 0.0 all-reduce.11.cloned.1.call-update
  98.2 0.0 all-reduce.9.cloned.1.call-start
  98.2 0.6 copy-done.5
  98.8 0.6 dynamic-slice
  100.1 164.4 %all-reduce.11.cloned.1.call-done = (bf16[9,640,640]{2,1,0:T(8,128)(2,1)}, bf16[3,640,640]{2,1,0:T(8,128)(2,1)}) async-done(((bf16[9,640,640]{2,1,0:T(8,128)(2,1)}, bf16[3,640,640]{2,1,0:T(8,128)(2,1)}), (bf16[9,640,640]{2,1,0:T(8,128)(2,1)}, bf16[3,640,640]{2,1,0:T(8,128)(2,1)})) %all-reduce.11.cloned.1.call-update) | async-done | bytes 9830416
  264.5 1.6 constant_dynamic-slice_fusion
  266.1 0.0 all-reduce.9.cloned.1.call-update
  266.1 0.0 all-gather.3.cloned.1.call-start
  266.2 1.8 constant_dynamic-slice_fusion.1
  268.0 0.0 all-gather.3.cloned.1.call-update
  268.0 101.2 %all-reduce.9.cloned.1.call-done = bf16[3,40,640]{2,1,0:T(8,128)(2,1)} async-done(((bf16[3,40,640]{2,1,0:T(8,128)(2,1)}), bf16[3,40,640]{2,1,0:T(8,128)(2,1)}) %all-reduce.9.cloned.1.call-update) | async-done | bytes 153616 | tf_op jit(solution)/shard_map/psum | solution.py:108
  369.2 1.7 fusion.21
  370.9 50.9 %all-gather.3.cloned.1.call-done = bf16[144,40,640]{2,1,0:T(8,128)(2,1)} async-done(((bf16[9,40,640]{2,1,0:T(8,128)(2,1)}), bf16[144,40,640]{2,1,0:T(8,128)(2,1)}) %all-gather.3.cloned.1.call-update) | async-done | bytes 7372816 | tf_op jit(solution)/shard_map/all_gather | solution.py:105
  421.8 4.4 reduce_sum.30
  426.2 0.8 fusion.5
  428.4 40.8 %psum.15 = f32[]{:T(128)} all-reduce(f32[]{:T(128)S(6)} %add.61), channel_id=1, replica_groups=mesh['dp'=16,'frame'=16] {'frame'}, use_global_device_ids=true, to_apply=%region_6.7 | all-reduce | flops 1 | bytes 8 | tf_op jit(solution)/shard_map/psum | solution.py:110
  469.9 2.1 fusion.6
  472.0 1.7 fusion.22
  (8 shorter events, 0.0 us)
Async XLA Ops:
  9.3 12.3 %copy-start.1 = (bf16[1,1,512,640]{3,2,1,0:T(8,128)(2,1)S(1)}, bf16[1,1,512,640]{3,2,1,0:T(8,128)(2,1)}, u32[]{:S(2)}) copy-start(bf16[1,1,512,640]{3,2,1,0:T(8,128)(2,1)} %param.5) | copy-start | bytes 1966084
  15.4 18.3 %all-to-all-start = ((bf16[16,2,10240]{2,1,0:T(2,128)(2,1)}), bf16[16,2,10240]{2,1,0:T(2,128)(2,1)S(1)}, u32[]{:S(2)}, u32[]{:S(2)}) async-start(bf16[16,2,10240]{2,1,0:T(2,128)(2,1)} %reshape.110), calls=%async_computation | async-start | bytes 1310720 | tf_op jit(solution)/shard_map/all_to_all | solution.py:86
  34.3 1.7 copy-start
  39.3 7.9 %copy-start.3 = (bf16[1,8,64,640]{3,2,1,0:T(8,128)(2,1)S(1)}, bf16[1,8,64,640]{3,2,1,0:T(8,128)(2,1)}, u32[]{:S(2)}) copy-start(bf16[1,8,64,640]{3,2,1,0:T(8,128)(2,1)} %get-tuple-element.15) | copy-start | bytes 1966084
  39.3 8.9 %copy-start.2 = (bf16[1,8,64,640]{3,2,1,0:T(8,128)(2,1)S(1)}, bf16[1,8,64,640]{3,2,1,0:T(8,128)(2,1)}, u32[]{:S(2)}) copy-start(bf16[1,8,64,640]{3,2,1,0:T(8,128)(2,1)} %get-tuple-element.16) | copy-start | bytes 1966084
  39.3 19.4 %all-to-all-start.1 = ((bf16[1,16,32,640]{3,2,0,1:T(8,128)(2,1)}), bf16[1,16,32,640]{3,2,0,1:T(8,128)(2,1)}, u32[]{:S(2)}, u32[]{:S(2)}) async-start(bf16[1,16,32,640]{3,2,0,1:T(8,128)(2,1)} %bitcast.19), calls=%async_computation.1 | async-start | bytes 1310720 | tf_op jit(solution)/shard_map/all_to_all | solution.py:91
  75.2 18.2 %all-to-all-start.2 = ((bf16[16,2,10240]{2,1,0:T(2,128)(2,1)}), bf16[16,2,10240]{2,1,0:T(2,128)(2,1)S(1)}, u32[]{:S(2)}, u32[]{:S(2)}) async-start(bf16[16,2,10240]{2,1,0:T(2,128)(2,1)} %reshape.112), calls=%async_computation.2 | async-start | bytes 1310720 | tf_op jit(solution)/shard_map/all_to_all | solution.py:85
  82.1 182.4 %all-reduce.11.cloned.1.call-start = ((), (), s32[]{:S(2)}) async-start(), calls=%async_computation.5 | async-start | bytes 19660800
  98.2 0.7 copy-start.5
  98.2 271.0 %all-reduce.9.cloned.1.call-start = ((), (), s32[]{:S(2)}) async-start(), calls=%async_computation.3 | async-start | bytes 307200 | tf_op jit(solution)/shard_map/psum | solution.py:108
  266.1 155.6 %all-gather.3.cloned.1.call-start = ((), (), s32[]{:S(2)}) async-start(), calls=%async_computation.4 | async-start | bytes 7833600 | tf_op jit(solution)/shard_map/all_gather | solution.py:105
  421.8 50.2 %copy-start.4 = (bf16[3,40,640]{2,1,0:T(8,128)(2,1)S(1)}, bf16[3,40,640]{2,1,0:T(8,128)(2,1)}, u32[]{:S(2)}) copy-start(bf16[3,40,640]{2,1,0:T(8,128)(2,1)} %all-reduce.9.cloned.1.call-done) | copy-start | bytes 460804
Sparse Core Ops, SparseCore 0:
  98.3 166.1 all-reduce.10
  267.4 101.7 all-reduce.8
  371.6 50.1 all-gather.2
